TPU v7x, 256 devices: a whole 4x4x8 slice. The times are simulated.
256 devices in a mesh: narrow: 16 (over z, core), wide: 16 (over x, y).
Axes of the slice: x: 4, y: 4, z: 8, core: 2. Of those that a mesh axis runs over, the one named last changes fastest.
Arguments:
- inputs: bfloat16 [2048, 8192], P('narrow', 'wide'), may hold values from -6 to 6
- gate_blocks: bfloat16 [112, 16, 128, 128], P('wide', 'narrow'), may hold values from -0.125 to 0.125
- up_blocks: bfloat16 [112, 16, 128, 128], P('wide', 'narrow'), may hold values from -0.125 to 0.125
- pattern: int32 [112, 16], P('wide'), may hold values from 0 to 63, as said below
- grad_hidden: bfloat16 [2048, 14336], P('narrow', 'wide'), may hold values from -0.59765625 to 0.59765625
Outputs:
- hidden: bfloat16 [2048, 14336], P('narrow', 'wide')
- grad_inputs: bfloat16 [2048, 8192], P('narrow', 'wide')
- grad_gate: bfloat16 [112, 16, 128, 128], P('wide', 'narrow')
- grad_up: bfloat16 [112, 16, 128, 128], P('wide', 'narrow')
Inputs may be any that keep to these rules, and one draw needn't show every extreme that they name: pattern[j, k] = b_j XOR m_k, with one offset b_j for each block column and 16 distinct masks m_k common to all block columns, so each block column lists 16 distinct block rows.
All inputs are finite; a program needn't handle non-finite values.
Results may differ from a plain program's by a relative error of at most 0.023.
Values may be sent and summed in bfloat16 or wider, within the bound.
A program may use at most 128 MiB of HBM per device.

v0:
```python
import jax
import jax.numpy as jnp
from jax import lax
from jax.sharding import PartitionSpec as P


def silu_parts(gate_sum):
    sigmoid_value = jax.nn.sigmoid(gate_sum)
    return (gate_sum * sigmoid_value, sigmoid_value * (1.0 + gate_sum * (1.0 - sigmoid_value)))


def shards(inputs, gate_blocks, up_blocks, pattern, grad_hidden):
    tokens_here = inputs.shape[0]
    block_size = gate_blocks.shape[2]
    columns = gate_blocks.shape[0]
    full_inputs = lax.all_gather(inputs, "wide", axis=1, tiled=True)
    row_blocks = full_inputs.shape[1] // block_size
    input_blocks = full_inputs.reshape(tokens_here, row_blocks, block_size)

    def picks_for():
        return jnp.take(input_blocks, pattern, axis=1)

    gate_all, up_all = (
        lax.all_gather(gate_blocks, "narrow", axis=1, tiled=True),
        lax.all_gather(up_blocks, "narrow", axis=1, tiled=True),
    )
    pieces = (gate_all, up_all)
    picked = picks_for()
    gate_sum = jnp.einsum("tjkb,jkbc->tjc", picked, pieces[0], preferred_element_type=jnp.float32)
    up_sum = jnp.einsum("tjkb,jkbc->tjc", picked, pieces[1], preferred_element_type=jnp.float32)
    gate_sum, up_sum = (gate_sum, up_sum)
    activation, derivative = silu_parts(gate_sum)
    hidden = (activation * up_sum).astype(jnp.bfloat16)
    cotangent = grad_hidden.reshape(tokens_here, columns, block_size).astype(jnp.float32)
    d_gate = (cotangent * up_sum * derivative).astype(jnp.bfloat16)
    d_up = (cotangent * activation).astype(jnp.bfloat16)
    zero_inputs = jnp.zeros((tokens_here, row_blocks, block_size), jnp.float32)
    pieces = (gate_all, up_all)
    number_slots = pieces[0].shape[1]

    def one_slot(k, running):
        gate_slot = lax.dynamic_index_in_dim(pieces[0], k, 1, keepdims=False)
        up_slot = lax.dynamic_index_in_dim(pieces[1], k, 1, keepdims=False)
        contribution = jnp.einsum(
            "tjc,jbc->tjb", d_gate, gate_slot, preferred_element_type=jnp.float32
        )
        contribution = contribution + jnp.einsum(
            "tjc,jbc->tjb", d_up, up_slot, preferred_element_type=jnp.float32
        )
        targets = lax.dynamic_index_in_dim(pattern, k, 1, keepdims=False)
        return running.at[:, targets].add(contribution)

    partial_inputs = lax.fori_loop(0, number_slots, one_slot, zero_inputs)
    grad_inputs = lax.psum_scatter(
        partial_inputs.reshape(tokens_here, row_blocks * block_size).astype(jnp.bfloat16),
        "wide",
        scatter_dimension=1,
        tiled=True,
    )
    picked_all = picks_for()
    gate_terms = jnp.einsum(
        "tjkb,tjc->jkbc", picked_all, d_gate, preferred_element_type=jnp.float32
    )
    up_terms = jnp.einsum("tjkb,tjc->jkbc", picked_all, d_up, preferred_element_type=jnp.float32)
    grad_gate, grad_up = (
        lax.psum_scatter(
            gate_terms.astype(jnp.bfloat16), "narrow", scatter_dimension=1, tiled=True
        ).astype(jnp.float32),
        lax.psum_scatter(
            up_terms.astype(jnp.bfloat16), "narrow", scatter_dimension=1, tiled=True
        ).astype(jnp.float32),
    )
    return (
        hidden.reshape(tokens_here, columns * block_size),
        grad_inputs,
        grad_gate.astype(jnp.bfloat16),
        grad_up.astype(jnp.bfloat16),
    )


def solution(mesh):
    placed = (
        P("narrow", "wide"),
        P("wide", "narrow", None, None),
        P("wide", "narrow", None, None),
        P("wide", None),
        P("narrow", "wide"),
    )
    return jax.shard_map(
        shards,
        mesh=mesh,
        in_specs=placed,
        out_specs=(
            P("narrow", "wide"),
            P("narrow", "wide"),
            P("wide", "narrow", None, None),
            P("wide", "narrow", None, None),
        ),
        check_vma=False,
    )
```

profile of v0, /device:TPU:32, one launch (start us, length us, event | category | flops | bytes accessed | tf_op | source)
XLA Modules:
  0.0 384.9 jit_solution(9591232748475014344)
XLA Ops:
  16.0 47.6 %all-gather.4.cloned.1.call-done = bf16[128,8192]{0,1:T(8,128)(2,1)} async-done(((bf16[128,512]{0,1:T(8,128)(2,1)}), bf16[128,8192]{0,1:T(8,128)(2,1)}) %all-gather.4.cloned.1.call-update) | async-done | bytes 2097168 | tf_op jit(solution)/shard_map/all_gather | solution.py:16
  63.6 3.2 copy.61
  66.8 3.0 gather_fusion
  69.8 6.1 %copy.62 = bf16[7,16,128,128]{2,3,1,0:T(8,128)(2,1)} copy(bf16[7,16,128,128]{3,2,1,0:T(8,128)(2,1)} %bitcast.89) | data formatting | bytes 7340032 | tf_op jit(solution)/shard_map/jit(_take)/gather | solution.py:21
  75.9 31.0 %all-gather.8.cloned.1.call-done = bf16[7,16,128,128]{2,3,1,0:T(8,128)(2,1)} async-done(((bf16[7,1,128,128]{2,3,1,0:T(8,128)(2,1)}), bf16[7,16,128,128]{2,3,1,0:T(8,128)(2,1)}) %all-gather.8.cloned.1.call-update) | async-done | bytes 3670032 | tf_op jit(solution)/shard_map/all_gather | solution.py:25
  106.9 4.4 %fusion.27 = f32[128,7,128]{0,2,1:T(8,128)S(1)} fusion(bf16[7,16,128,128]{2,3,1,0:T(8,128)(2,1)} %all-gather.8.cloned.1.call-done, bf16[7,16,128,128]{2,3,1,0:T(8,128)(2,1)} %copy.62, pred[7,16]{1,0:T(8,128)(4,1)S(1)} %compare_and_fusion), kind=kOutput, calls=%fused_computation.31 | convolution fusion | flops 471597056 | bytes 7798896 | tf_op jit(solution)/shard_map/tjkb,jkbc->tjc/dot_general | solution.py:30
  111.3 38.3 %all-gather.6.cloned.1.call-done = bf16[7,16,128,128]{2,3,1,0:T(8,128)(2,1)} async-done(((bf16[7,1,128,128]{2,3,1,0:T(8,128)(2,1)}), bf16[7,16,128,128]{2,3,1,0:T(8,128)(2,1)}) %all-gather.6.cloned.1.call-update) | async-done | bytes 3670032 | tf_op jit(solution)/shard_map/all_gather | solution.py:24
  149.6 4.5 %multiply_convert_fusion = (bf16[128,7,128]{0,2,1:T(8,128)(2,1)S(1)}, bf16[128,7,128]{0,2,1:T(8,128)(2,1)S(1)}, bf16[128,7,128]{0,2,1:T(8,128)(2,1)S(1)}) fusion(f32[128,7,128]{0,2,1:T(8,128)S(1)} %bitcast.91, f32[128,7,128]{0,2,1:T(8,128)S(1)} %fusion.27, bf16[7,16,128,128]{2,3,1,0:T(8,128)(2,1)} %all-gather.6.cloned.1.call-done, ...), kind=kOutput, calls=%fused_computation.33 | convolution fusion | flops 473317376 | bytes 8945776 | tf_op jit(solution)/shard_map/tjkb,jkbc->tjc/dot_general | solution.py:29
  154.3 5.1 %fusion.17 = bf16[7,16,128,128]{3,2,1,0:T(8,128)(2,1)} fusion(bf16[7,16,128,128]{2,3,1,0:T(8,128)(2,1)} %copy.62, pred[7,16]{1,0:T(8,128)(4,1)S(1)} %compare_and_fusion, bf16[128,7,128]{0,2,1:T(8,128)(2,1)S(1)} %get-tuple-element.191), kind=kOutput, calls=%fused_computation.23 | convolution fusion | flops 473432064 | bytes 7569520 | tf_op jit(solution)/shard_map/tjkb,tjc->jkbc/dot_general | solution.py:61
  159.6 5.0 %fusion.20 = bf16[7,16,128,128]{3,2,1,0:T(8,128)(2,1)} fusion(bf16[7,16,128,128]{2,3,1,0:T(8,128)(2,1)} %copy.62, pred[7,16]{1,0:T(8,128)(4,1)S(1)} %compare_and_fusion, bf16[128,7,128]{0,2,1:T(8,128)(2,1)S(1)} %get-tuple-element.190), kind=kOutput, calls=%fused_computation.24 | convolution fusion | flops 473432064 | bytes 7569520 | tf_op jit(solution)/shard_map/tjkb,tjc->jkbc/dot_general | solution.py:64
  164.7 2.5 broadcast_in_dim.15
  167.1 86.0 %while.13 = (s32[]{:T(128)}, f32[128,64,128]{2,0,1:T(8,128)}, s32[7,16]{0,1:T(8,128)S(1)}, bf16[7,16,128,128]{2,3,1,0:T(8,128)(2,1)}, bf16[128,7,128]{2,0,1:T(8,...) while((s32[]{:T(128)}, f32[128,64,128]{2,0,1:T(8,128)}, ...), condition=%wide.region_2.4_spmd, body=%wide.region_0.3_spmd.sunk | while | flops 58949656 | bytes 4587709 | solution.py:53
  169.9 2.6 scatter_fusion
  175.2 2.7 scatter_fusion
  180.6 2.7 scatter_fusion
  186.0 2.7 scatter_fusion
  191.4 2.7 scatter_fusion
  196.8 2.7 scatter_fusion
  202.1 2.7 scatter_fusion
  207.5 2.7 scatter_fusion
  212.9 2.6 scatter_fusion
  218.3 2.6 scatter_fusion
  223.6 2.6 scatter_fusion
  229.0 2.6 scatter_fusion
  234.3 2.6 scatter_fusion
  239.7 2.7 scatter_fusion
  245.1 2.7 scatter_fusion
  250.5 2.7 scatter_fusion
  253.1 3.9 %copy_bitcast_fusion = bf16[128,8192]{1,0:T(8,128)(2,1)} fusion(f32[128,64,128]{2,0,1:T(8,128)} %get-tuple-element.129), kind=kLoop, calls=%fused_computation.25 | loop fusion | flops 1048576 | bytes 6291456 | tf_op jit(solution)/shard_map/convert_element_type | solution.py:55
  258.5 34.1 %all-reduce.5.cloned.1.call-done = (bf16[7,16,128,128]{3,2,1,0:T(8,128)(2,1)}, bf16[7,16,128,128]{3,2,1,0:T(8,128)(2,1)}) async-done(((bf16[7,16,128,128]{3,2,1,0:T(8,128)(2,1)}, bf16[7,16,128,128]{3,2,1,0:T(8,128)(2,1)}), (bf16[7,16,128,128]{3,2,1,0:T(8,128)(2,1)}, bf16[7,16,128,128]{3,2,1,0:T(8,128)(2,1)})) %all-reduce.5.cloned.1.call-update) | async-done | bytes 7340048
  292.6 2.5 constant_dynamic-slice_fusion.1
  295.1 83.3 %reduce-scatter.8.cloned.1.call-done = bf16[128,512]{1,0:T(8,128)(2,1)} async-done(((bf16[128,8192]{1,0:T(8,128)(2,1)}), bf16[128,512]{1,0:T(8,128)(2,1)}) %reduce-scatter.8.cloned.1.call-update) | async-done | bytes 131088 | tf_op jit(solution)/shard_map/reduce_scatter | solution.py:54
  (89 shorter events, 54.1 us)
Async XLA Ops:
  7.2 56.4 %all-gather.4.cloned.1.call-start = ((), (), s32[]{:S(2)}) async-start(), calls=%async_computation.1 | async-start | bytes 2228224 | tf_op jit(solution)/shard_map/all_gather | solution.py:16
  8.9 98.0 %all-gather.8.cloned.1.call-start = ((), (), s32[]{:S(2)}) async-start(), calls=%async_computation.3 | async-start | bytes 3899392 | tf_op jit(solution)/shard_map/all_gather | solution.py:25
  10.7 138.8 %all-gather.6.cloned.1.call-start = ((), (), s32[]{:S(2)}) async-start(), calls=%async_computation.2 | async-start | bytes 3899392 | tf_op jit(solution)/shard_map/all_gather | solution.py:24
  12.6 280.0 %all-reduce.5.cloned.1.call-start = ((), (), s32[]{:S(2)}) async-start(), calls=%async_computation.5 | async-start | bytes 14680064
  164.6 213.7 %reduce-scatter.8.cloned.1.call-start = ((), (), s32[]{:S(2)}) async-start(), calls=%async_computation.4 | async-start | bytes 2228224 | tf_op jit(solution)/shard_map/reduce_scatter | solution.py:54
  253.1 3.9 %copy-start = (u32[256]{0:T(256)S(1)}, u32[256]{0:T(256)}, u32[]{:S(2)}) copy-start(u32[256]{0:T(256)} %constant.58) | copy-start | bytes 3076
Sparse Core Ops, SparseCore 0:
  11.0 52.5 all-gather.3
  66.0 40.8 all-gather.7
  109.3 40.2 all-gather.5
  164.7 127.8 all-reduce.4
  296.6 81.7 reduce-scatter.7
where the time goes:
time: 387 us; the launch traced here: 385 us
  waiting for transfers between devices  234 us (60%)
  matrix products  59.2 us (15%)
  other arithmetic  47.8 us (12%)
  local copies, waits for them, and re-layouts  29.3 us (8%)
  between operations  13.8 us (4%)
    reduce_scatter x1, waiting for transfers between devices, shards(): lax.psum_scatter(partial_inputs.reshape(tokens_here, row_blocks * block_s...  83.3 us
    all_gather x1, waiting for transfers between devices, shards(): full_inputs = lax.all_gather(inputs, 'wide', axis=1, tiled=True)  47.6 us
    scatter-add x16, other arithmetic, one_slot(): return running.at[:, targets].add(contribution)  42.4 us
    all_gather x1, waiting for transfers between devices, shards(): lax.all_gather(gate_blocks, 'narrow', axis=1, tiled=True)  38.3 us
    unnamed x6, waiting for transfers between devices  34.2 us
    all_gather x1, waiting for transfers between devices, shards(): lax.all_gather(up_blocks, 'narrow', axis=1, tiled=True)  31 us
    dot_general x16, matrix products, one_slot(): jnp.einsum('tjc,jbc->tjb', d_up, up_slot, preferred_element_type=jnp.floa...  20.2 us
    dot_general x16, matrix products, one_slot(): jnp.einsum('tjc,jbc->tjb', d_gate, gate_slot, preferred_element_type=jnp....  20 us
  transfers between devices with their start and end apart: 5, of which 5 were waited for; matrix products, arithmetic and copies ran while one was open for 31% of the time, Pallas kernels for 0%

commit v1 on v0

--- a/solution.py
+++ b/solution.py
@@ -2,6 +2,12 @@
 import jax.numpy as jnp
 from jax import lax
 from jax.sharding import PartitionSpec as P
+
+
+def carry_slots_on(x_in, dim_k):
+    x_in = jnp.moveaxis(x_in, 0, dim_k)
+    top = x_in.shape
+    return x_in.reshape(*top[:dim_k], top[dim_k] * top[dim_k + 1], *top[dim_k + 2 :])
 
 
 def silu_parts(gate_sum):
@@ -20,9 +26,30 @@
     def picks_for():
         return jnp.take(input_blocks, pattern, axis=1)
 
+    def produce_works(dev_axis, dim_i, block_in):
+        p_count = lax.axis_size(dev_axis)
+        so_far_all = []
+        for idx in [*range(p_count)]:
+            so_far_all.append((idx, (idx + 1) % p_count))
+        buffer = []
+        for d, to_i in so_far_all:
+            buffer.append((to_i, d))
+        f_next, h_now = ([], [])
+        for ii in [*range(p_count - 1)]:
+            if ii % 2 == 0:
+                f_next.append(
+                    lax.ppermute(f_next[-1] if f_next else block_in, dev_axis, so_far_all)
+                )
+            else:
+                h_now.append(lax.ppermute(h_now[-1] if h_now else block_in, dev_axis, buffer))
+        near = jnp.stack([*f_next[::-1], block_in, *h_now])
+        upper = lax.axis_index(dev_axis) - len(f_next)
+        near = near[(jnp.arange(p_count) - upper) % p_count]
+        return carry_slots_on(near, dim_i)
+
     gate_all, up_all = (
         lax.all_gather(gate_blocks, "narrow", axis=1, tiled=True),
-        lax.all_gather(up_blocks, "narrow", axis=1, tiled=True),
+        produce_works("narrow", 1, up_blocks),
     )
     pieces = (gate_all, up_all)
     picked = picks_for()

time: 387 us -> 348 us (0.90)
  waiting for transfers between devices: 234 us -> 164 us
  local copies, waits for them, and re-layouts: 29.3 us -> 46.6 us
  starting transfers between devices: 0.21 us -> 16.8 us
    all_gather x1, waiting for transfers between devices: 47.6 us -> 0.01 us  [shards(): full_inputs = lax.all_gather(inputs, 'wide', axis=1, tiled=True)]
    all_gather x1 -> x0, waiting for transfers between devices: 31 us -> none  [shards(): lax.all_gather(up_blocks, 'narrow', axis=1, tiled=True)]
    ppermute x0 -> x15, waiting for transfers between devices: none -> 27.9 us  [the longest x8 25.6 us: produce_works(): lax.ppermute(f_next[-1] if f_next else block_in, dev_axis, so_far_all)]
    all_gather x1, waiting for transfers between devices: 38.3 us -> 17.8 us  [shards(): lax.all_gather(gate_blocks, 'narrow', axis=1, tiled=True)]
    ppermute x0 -> x15, starting transfers between devices: none -> 16.6 us  [the longest x7 16.6 us: produce_works(): lax.ppermute(h_now[-1] if h_now else block_in, dev_axis, buffer)]
    unnamed x8 -> x28, local copies, waits for them, and re-layouts: 9.13 us -> 20.8 us
    gather x0 -> x1, local copies, waits for them, and re-layouts: none -> 4.93 us  [produce_works(): near = near[(jnp.arange(p_count) - upper) % p_count]]
    unnamed x6 -> x5, waiting for transfers between devices: 34.2 us -> 34.7 us
  transfers between devices with their start and end apart: 5 -> 19, of which waited for: 5 -> 15; matrix products, arithmetic and copies ran while one was open for 31% -> 38% of each run, Pallas kernels for 0% -> 0%
where the time goes in v1:
time: 348 us; the launch traced here: 345 us
  waiting for transfers between devices  164 us (47%)
  matrix products  56.4 us (16%)
  other arithmetic  47.8 us (14%)
  local copies, waits for them, and re-layouts  46.6 us (13%)
  starting transfers between devices  16.8 us (5%)
  between operations  13.9 us (4%)
    reduce_scatter x1, waiting for transfers between devices, shards(): lax.psum_scatter(partial_inputs.reshape(tokens_here, row_blocks * block_s...  83.3 us
    scatter-add x16, other arithmetic, one_slot(): return running.at[:, targets].add(contribution)  42.4 us
    unnamed x5, waiting for transfers between devices  34.7 us
    ppermute x8, waiting for transfers between devices, produce_works(): lax.ppermute(f_next[-1] if f_next else block_in, dev_axis, so_far_all)  25.6 us
    unnamed x28, local copies, waits for them, and re-layouts  20.8 us
    dot_general x16, matrix products, one_slot(): jnp.einsum('tjc,jbc->tjb', d_gate, gate_slot, preferred_element_type=jnp....  20 us
    dot_general x16, matrix products, one_slot(): jnp.einsum('tjc,jbc->tjb', d_up, up_slot, preferred_element_type=jnp.floa...  19.7 us
    all_gather x1, waiting for transfers between devices, shards(): lax.all_gather(gate_blocks, 'narrow', axis=1, tiled=True)  17.8 us
  transfers between devices with their start and end apart: 19, of which 15 were waited for; matrix products, arithmetic and copies ran while one was open for 38% of the time, Pallas kernels for 0%

profile of v1, /device:TPU:32, one launch (start us, length us, event | category | flops | bytes accessed | tf_op | source)
XLA Modules:
  0.0 345.2 jit_solution(16476054038144201564)
XLA Ops:
  10.9 5.6 %collective-permute-done = bf16[7,1,128,128]{3,2,1,0:T(8,128)(2,1)S(1)} collective-permute-done((bf16[7,1,128,128]{3,2,1,0:T(8,128)(2,1)}, bf16[7,1,128,128]{3,2,1,0:T(8,128)(2,1)S(1)}, u32[]{:S(2)}, u32[]{:S(2)}) %collective-permute-start) | collective-permute-done | bytes 229408 | tf_op jit(solution)/shard_map/ppermute | solution.py:41
  18.3 3.7 %collective-permute-done.1 = bf16[7,1,128,128]{3,2,0,1:T(8,128)(2,1)S(1)} collective-permute-done((bf16[7,1,128,128]{3,2,0,1:T(8,128)(2,1)S(1)}, bf16[7,1,128,128]{3,2,0,1:T(8,128)(2,1)S(1)}, u32[]{:S(2)}, u32[]{:S(2)}) %collective-permute-start.1) | collective-permute-done | bytes 229408 | tf_op jit(solution)/shard_map/ppermute | solution.py:41
  24.2 3.2 collective-permute-done.2
  30.0 2.9 collective-permute-done.3
  41.6 3.3 collective-permute-done.5
  45.8 3.0 collective-permute-start.13
  48.7 3.0 collective-permute-done.6
  54.3 3.0 collective-permute-start.14
  72.0 4.9 %gather_fusion = bf16[16,7,128,128]{3,2,1,0:T(8,128)(2,1)} fusion(bf16[16,7,128,128]{3,2,1,0:T(8,128)(2,1)} %bitcast.29, s32[1024]{0:T(1024)S(1)} %pad_clamp_fusion), kind=kCustom, calls=%fused_computation.1 | custom fusion | bytes 7340096 | tf_op jit(solution)/shard_map/gather | solution.py:47
  76.9 3.2 copy.64
  80.1 2.9 gather_fusion.1
  83.1 6.1 %copy.65 = bf16[7,16,128,128]{2,3,1,0:T(8,128)(2,1)} copy(bf16[7,16,128,128]{3,2,1,0:T(8,128)(2,1)} %bitcast.129) | data formatting | bytes 7340032 | tf_op jit(solution)/shard_map/jit(_take)/gather | solution.py:27
  89.1 17.8 %all-gather.5.cloned.1.call-done = bf16[7,16,128,128]{2,3,1,0:T(8,128)(2,1)} async-done(((bf16[7,1,128,128]{2,3,1,0:T(8,128)(2,1)}), bf16[7,16,128,128]{2,3,1,0:T(8,128)(2,1)}) %all-gather.5.cloned.1.call-update) | async-done | bytes 3670032 | tf_op jit(solution)/shard_map/all_gather | solution.py:51
  106.9 4.5 %convolution_bitcast_fusion = f32[128,7,128]{0,2,1:T(8,128)S(1)} fusion(bf16[7,16,128,128]{2,3,1,0:T(8,128)(2,1)} %all-gather.5.cloned.1.call-done, bf16[7,16,128,128]{2,3,1,0:T(8,128)(2,1)} %copy.65, pred[7,16]{1,0:T(8,128)(4,1)S(1)} %compare_and_fusion), kind=kOutput, calls=%fused_computation.23 | convolution fusion | flops 471597056 | bytes 7798896 | tf_op jit(solution)/shard_map/tjkb,jkbc->tjc/dot_general | solution.py:56
  114.4 5.1 %convolution_convert_fusion.1 = bf16[7,16,128,128]{3,2,1,0:T(8,128)(2,1)} fusion(bf16[128,7,128]{0,2,1:T(8,128)(2,1)S(1)} %get-tuple-element.191, bf16[7,16,128,128]{2,3,1,0:T(8,128)(2,1)} %copy.65, pred[7,16]{1,0:T(8,128)(4,1)S(1)} %compare_and_fusion), kind=kOutput, calls=%fused_computation.19 | convolution fusion | flops 473432064 | bytes 7569520 | tf_op jit(solution)/shard_map/tjkb,tjc->jkbc/dot_general | solution.py:88
  119.7 5.0 %convolution_convert_fusion = bf16[7,16,128,128]{3,2,1,0:T(8,128)(2,1)} fusion(bf16[128,7,128]{0,2,1:T(8,128)(2,1)S(1)} %get-tuple-element.190, bf16[7,16,128,128]{2,3,1,0:T(8,128)(2,1)} %copy.65, pred[7,16]{1,0:T(8,128)(4,1)S(1)} %compare_and_fusion), kind=kOutput, calls=%fused_computation.18 | convolution fusion | flops 473432064 | bytes 7569520 | tf_op jit(solution)/shard_map/tjkb,tjc->jkbc/dot_general | solution.py:91
  127.2 85.5 %while.13 = (s32[]{:T(128)}, f32[128,64,128]{2,0,1:T(8,128)}, s32[7,16]{0,1:T(8,128)S(1)}, bf16[7,16,128,128]{2,3,1,0:T(8,128)(2,1)}, bf16[128,7,128]{2,0,1:T(8,...) while((s32[]{:T(128)}, f32[128,64,128]{2,0,1:T(8,128)}, ...), condition=%wide.region_2.4_spmd, body=%wide.region_0.3_spmd.sunk | while | flops 58949656 | bytes 4587709 | solution.py:80
  129.9 2.6 scatter_fusion
  135.3 2.7 scatter_fusion
  140.6 2.7 scatter_fusion
  146.0 2.7 scatter_fusion
  151.3 2.7 scatter_fusion
  156.7 2.6 scatter_fusion
  167.4 2.7 scatter_fusion
  172.7 2.7 scatter_fusion
  188.7 2.6 scatter_fusion
  194.1 2.6 scatter_fusion
  199.4 2.6 scatter_fusion
  204.8 2.7 scatter_fusion
  212.7 3.9 %copy_bitcast_fusion = bf16[128,8192]{1,0:T(8,128)(2,1)} fusion(f32[128,64,128]{2,0,1:T(8,128)} %get-tuple-element.129), kind=kLoop, calls=%fused_computation.20 | loop fusion | flops 1048576 | bytes 6291456 | tf_op jit(solution)/shard_map/convert_element_type | solution.py:82
  218.2 34.6 %all-reduce.5.cloned.1.call-done = (bf16[7,16,128,128]{3,2,1,0:T(8,128)(2,1)}, bf16[7,16,128,128]{3,2,1,0:T(8,128)(2,1)}) async-done(((bf16[7,16,128,128]{3,2,1,0:T(8,128)(2,1)}, bf16[7,16,128,128]{3,2,1,0:T(8,128)(2,1)}), (bf16[7,16,128,128]{3,2,1,0:T(8,128)(2,1)}, bf16[7,16,128,128]{3,2,1,0:T(8,128)(2,1)})) %all-reduce.5.cloned.1.call-update) | async-done | bytes 7340048
  255.4 83.3 %reduce-scatter.8.cloned.1.call-done = bf16[128,512]{1,0:T(8,128)(2,1)} async-done(((bf16[128,8192]{1,0:T(8,128)(2,1)}), bf16[128,512]{1,0:T(8,128)(2,1)}) %reduce-scatter.8.cloned.1.call-update) | async-done | bytes 131088 | tf_op jit(solution)/shard_map/reduce_scatter | solution.py:81
  (140 shorter events, 100.4 us)
Async XLA Ops:
  7.2 59.1 %copy-start.2 = (bf16[7,1,128,128]{3,2,1,0:T(8,128)(2,1)S(1)}, bf16[7,1,128,128]{3,2,1,0:T(8,128)(2,1)}, u32[]{:S(2)}) copy-start(bf16[7,1,128,128]{3,2,1,0:T(8,128)(2,1)} %param.11) | copy-start | bytes 688132
  7.2 69.7 %all-gather.3.cloned.1.call-start = ((), (), s32[]{:S(2)}) async-start(), calls=%async_computation.1 | async-start | bytes 2228224 | tf_op jit(solution)/shard_map/all_gather | solution.py:22
  9.0 98.0 %all-gather.5.cloned.1.call-start = ((), (), s32[]{:S(2)}) async-start(), calls=%async_computation.2 | async-start | bytes 3899392 | tf_op jit(solution)/shard_map/all_gather | solution.py:51
  10.8 242.0 %all-reduce.5.cloned.1.call-start = ((), (), s32[]{:S(2)}) async-start(), calls=%async_computation.4 | async-start | bytes 14680064
  10.9 5.7 %collective-permute-start = (bf16[7,1,128,128]{3,2,1,0:T(8,128)(2,1)}, bf16[7,1,128,128]{3,2,1,0:T(8,128)(2,1)S(1)}, u32[]{:S(2)}, u32[]{:S(2)}) collective-permute-start(bf16[7,1,128,128]{3,2,1,0:T(8,128)(2,1)} %param.11), channel_id=1, source_target_pairs={{0,16},{16,32},{32,48},{48,64},{64,80},{80,96},{96,112},{112,128},... | collective-permute-start | bytes 688136 | tf_op jit(solution)/shard_map/ppermute | solution.py:41
  16.5 5.4 %collective-permute-start.1 = (bf16[7,1,128,128]{3,2,0,1:T(8,128)(2,1)S(1)}, bf16[7,1,128,128]{3,2,0,1:T(8,128)(2,1)S(1)}, u32[]{:S(2)}, u32[]{:S(2)}) collective-permute-start(bf16[7,1,128,128]{3,2,0,1:T(8,128)(2,1)S(1)} %bitcast.134), channel_id=1, source_target_pairs={{0,16},{16,32},{32,48},{48,64},{64,80},{80,96},{96,112},{112,128},... | collective-permute-start | bytes 688136 | tf_op jit(solution)/shard_map/ppermute | solution.py:41
  16.5 5.6 %collective-permute-start.8 = (bf16[7,1,128,128]{3,2,0,1:T(8,128)(2,1)}, bf16[7,1,128,128]{3,2,0,1:T(8,128)(2,1)S(1)}, u32[]{:S(2)}, u32[]{:S(2)}) collective-permute-start(bf16[7,1,128,128]{3,2,0,1:T(8,128)(2,1)} %bitcast.133), channel_id=1, source_target_pairs={{16,0},{32,16},{48,32},{64,48},{80,64},{96,80},{112,96},{128,112},... | collective-permute-start | bytes 688136 | tf_op jit(solution)/shard_map/ppermute | solution.py:44
  22.0 5.4 %collective-permute-start.2 = (bf16[7,1,128,128]{3,2,0,1:T(8,128)(2,1)S(1)}, bf16[7,1,128,128]{3,2,0,1:T(8,128)(2,1)S(1)}, u32[]{:S(2)}, u32[]{:S(2)}) collective-permute-start(bf16[7,1,128,128]{3,2,0,1:T(8,128)(2,1)S(1)} %collective-permute-done.1), channel_id=1, source_target_pairs={{0,16},{16,32},{32,48},{48,64},{64,80},{80,96},{96,112},{112,128},... | collective-permute-start | bytes 688136 | tf_op jit(solution)/shard_map/ppermute | solution.py:41
  22.1 5.6 %collective-permute-start.9 = (bf16[7,1,128,128]{3,2,0,1:T(8,128)(2,1)S(1)}, bf16[7,1,128,128]{3,2,0,1:T(8,128)(2,1)S(1)}, u32[]{:S(2)}, u32[]{:S(2)}) collective-permute-start(bf16[7,1,128,128]{3,2,0,1:T(8,128)(2,1)S(1)} %collective-permute-done.8), channel_id=1, source_target_pairs={{16,0},{32,16},{48,32},{64,48},{80,64},{96,80},{112,96},{128,112},... | collective-permute-start | bytes 688136 | tf_op jit(solution)/shard_map/ppermute | solution.py:44
  27.4 5.4 %collective-permute-start.3 = (bf16[7,1,128,128]{3,2,0,1:T(8,128)(2,1)S(1)}, bf16[7,1,128,128]{3,2,0,1:T(8,128)(2,1)S(1)}, u32[]{:S(2)}, u32[]{:S(2)}) collective-permute-start(bf16[7,1,128,128]{3,2,0,1:T(8,128)(2,1)S(1)} %collective-permute-done.2), channel_id=1, source_target_pairs={{0,16},{16,32},{32,48},{48,64},{64,80},{80,96},{96,112},{112,128},... | collective-permute-start | bytes 688136 | tf_op jit(solution)/shard_map/ppermute | solution.py:41
  27.8 5.8 %collective-permute-start.10 = (bf16[7,1,128,128]{3,2,0,1:T(8,128)(2,1)S(1)}, bf16[7,1,128,128]{3,2,0,1:T(8,128)(2,1)S(1)}, u32[]{:S(2)}, u32[]{:S(2)}) collective-permute-start(bf16[7,1,128,128]{3,2,0,1:T(8,128)(2,1)S(1)} %collective-permute-done.9), channel_id=1, source_target_pairs={{16,0},{32,16},{48,32},{64,48},{80,64},{96,80},{112,96},{128,112},... | collective-permute-start | bytes 688136 | tf_op jit(solution)/shard_map/ppermute | solution.py:44
  32.9 5.4 %collective-permute-start.4 = (bf16[7,1,128,128]{3,2,0,1:T(8,128)(2,1)S(1)}, bf16[7,1,128,128]{3,2,0,1:T(8,128)(2,1)S(1)}, u32[]{:S(2)}, u32[]{:S(2)}) collective-permute-start(bf16[7,1,128,128]{3,2,0,1:T(8,128)(2,1)S(1)} %collective-permute-done.3), channel_id=1, source_target_pairs={{0,16},{16,32},{32,48},{48,64},{64,80},{80,96},{96,112},{112,128},... | collective-permute-start | bytes 688136 | tf_op jit(solution)/shard_map/ppermute | solution.py:41
  33.5 5.8 %collective-permute-start.11 = (bf16[7,1,128,128]{3,2,0,1:T(8,128)(2,1)S(1)}, bf16[7,1,128,128]{3,2,0,1:T(8,128)(2,1)S(1)}, u32[]{:S(2)}, u32[]{:S(2)}) collective-permute-start(bf16[7,1,128,128]{3,2,0,1:T(8,128)(2,1)S(1)} %collective-permute-done.10), channel_id=1, source_target_pairs={{16,0},{32,16},{48,32},{64,48},{80,64},{96,80},{112,96},{128,112},... | collective-permute-start | bytes 688136 | tf_op jit(solution)/shard_map/ppermute | solution.py:44
  38.3 6.7 %collective-permute-start.5 = (bf16[7,1,128,128]{3,2,0,1:T(8,128)(2,1)S(1)}, bf16[7,1,128,128]{3,2,0,1:T(8,128)(2,1)S(1)}, u32[]{:S(2)}, u32[]{:S(2)}) collective-permute-start(bf16[7,1,128,128]{3,2,0,1:T(8,128)(2,1)S(1)} %collective-permute-done.4), channel_id=1, source_target_pairs={{0,16},{16,32},{32,48},{48,64},{64,80},{80,96},{96,112},{112,128},... | collective-permute-start | bytes 688136 | tf_op jit(solution)/shard_map/ppermute | solution.py:41
  39.4 6.4 %collective-permute-start.12 = (bf16[7,1,128,128]{3,2,0,1:T(8,128)(2,1)S(1)}, bf16[7,1,128,128]{3,2,0,1:T(8,128)(2,1)S(1)}, u32[]{:S(2)}, u32[]{:S(2)}) collective-permute-start(bf16[7,1,128,128]{3,2,0,1:T(8,128)(2,1)S(1)} %collective-permute-done.11), channel_id=1, source_target_pairs={{16,0},{32,16},{48,32},{64,48},{80,64},{96,80},{112,96},{128,112},... | collective-permute-start | bytes 688136 | tf_op jit(solution)/shard_map/ppermute | solution.py:44
  45.0 6.8 %collective-permute-start.6 = (bf16[7,1,128,128]{3,2,0,1:T(8,128)(2,1)S(1)}, bf16[7,1,128,128]{3,2,0,1:T(8,128)(2,1)}, u32[]{:S(2)}, u32[]{:S(2)}) collective-permute-start(bf16[7,1,128,128]{3,2,0,1:T(8,128)(2,1)S(1)} %collective-permute-done.5), channel_id=1, source_target_pairs={{0,16},{16,32},{32,48},{48,64},{64,80},{80,96},{96,112},{112,128},... | collective-permute-start | bytes 688136 | tf_op jit(solution)/shard_map/ppermute | solution.py:41
  45.8 8.5 %collective-permute-start.13 = (bf16[7,1,128,128]{3,2,0,1:T(8,128)(2,1)S(1)}, bf16[7,1,128,128]{3,2,0,1:T(8,128)(2,1)S(1)}, u32[]{:S(2)}, u32[]{:S(2)}) collective-permute-start(bf16[7,1,128,128]{3,2,0,1:T(8,128)(2,1)S(1)} %collective-permute-done.12), channel_id=1, source_target_pairs={{16,0},{32,16},{48,32},{64,48},{80,64},{96,80},{112,96},{128,112},... | collective-permute-start | bytes 688136 | tf_op jit(solution)/shard_map/ppermute | solution.py:44
  51.7 7.0 %collective-permute-start.7 = (bf16[7,1,128,128]{3,2,0,1:T(8,128)(2,1)}, bf16[7,1,128,128]{3,2,0,1:T(8,128)(2,1)}, u32[]{:S(2)}, u32[]{:S(2)}) collective-permute-start(bf16[7,1,128,128]{3,2,0,1:T(8,128)(2,1)} %collective-permute-done.6), channel_id=1, source_target_pairs={{0,16},{16,32},{32,48},{48,64},{64,80},{80,96},{96,112},{112,128},... | collective-permute-start | bytes 688136 | tf_op jit(solution)/shard_map/ppermute | solution.py:41
  54.3 17.0 %collective-permute-start.14 = (bf16[7,1,128,128]{3,2,0,1:T(8,128)(2,1)S(1)}, bf16[7,1,128,128]{3,2,0,1:T(8,128)(2,1)S(1)}, u32[]{:S(2)}, u32[]{:S(2)}) collective-permute-start(bf16[7,1,128,128]{3,2,0,1:T(8,128)(2,1)S(1)} %collective-permute-done.13), channel_id=1, source_target_pairs={{16,0},{32,16},{48,32},{64,48},{80,64},{96,80},{112,96},{128,112},... | collective-permute-start | bytes 688136 | tf_op jit(solution)/shard_map/ppermute | solution.py:44
  106.9 4.5 %copy-start = (bf16[16,7,128,128]{3,2,1,0:T(8,128)(2,1)S(1)}, bf16[16,7,128,128]{3,2,1,0:T(8,128)(2,1)}, u32[]{:S(2)}) copy-start(bf16[16,7,128,128]{3,2,1,0:T(8,128)(2,1)} %gather_fusion) | copy-start | bytes 11010052
  106.9 5.3 %copy-start.1 = (bf16[7,16,128,128]{2,3,1,0:T(8,128)(2,1)S(1)}, bf16[7,16,128,128]{2,3,1,0:T(8,128)(2,1)}, u32[]{:S(2)}) copy-start(bf16[7,16,128,128]{2,3,1,0:T(8,128)(2,1)} %copy.65) | copy-start | bytes 11010052
  124.7 213.9 %reduce-scatter.8.cloned.1.call-start = ((), (), s32[]{:S(2)}) async-start(), calls=%async_computation.3 | async-start | bytes 2228224 | tf_op jit(solution)/shard_map/reduce_scatter | solution.py:81
  212.7 4.0 %copy-start.3 = (u32[256]{0:T(256)S(1)}, u32[256]{0:T(256)}, u32[]{:S(2)}) copy-start(u32[256]{0:T(256)} %constant.82) | copy-start | bytes 3076
Sparse Core Ops, SparseCore 0:
  11.0 52.5 all-gather.2
  66.0 40.8 all-gather.4
  124.8 127.9 all-reduce.4
  256.8 81.7 reduce-scatter.7
